TPU v7x, 128 devices: a whole 4x4x4 slice. The times are simulated.
128 devices in a mesh: rows: 32 (over x, z, y_lo), cols: 4 (over y_hi, core).
Axes of the slice: x: 4, y: 4 (y_hi: 2, y_lo: 2; y = y_hi * 2 + y_lo), z: 4, core: 2. Of those that a mesh axis runs over, the one named last changes fastest.
Arguments:
- vectors: bfloat16 [131072, 1024], P('rows'), may hold values from -6 to 6
- near_tiles: bfloat16 [512, 16, 256, 256], P(('rows', 'cols')), may hold values from -0.09375 to 0.09375
- near_cols: int32 [512, 16], P(('rows', 'cols')), may hold values from 0 to 19, as said below
- left_one: bfloat16 [131072, 512], P('rows', 'cols'), may hold values from -0.25 to 0.25
- right_one: bfloat16 [131072, 512], P('rows', 'cols'), may hold values from -0.0234375 to 0.0234375
- left_two: bfloat16 [131072, 512], P('rows', 'cols'), may hold values from -0.25 to 0.25
- right_two: bfloat16 [131072, 512], P('rows', 'cols'), may hold values from -0.03125 to 0.03125
Outputs:
- product: bfloat16 [131072, 1024], P(('rows', 'cols'))
Inputs may be any that keep to these rules, and one draw needn't show every extreme that they name: `near_cols`: each row names 16 different column tiles of its window of 20.
All inputs are finite; a program needn't handle non-finite values.
Results may differ from a plain program's by a relative error of at most 0.014.
Values may be sent and summed in bfloat16 or wider, within the bound.
A program may use at most 192 MiB of HBM per device.

v0:
```python
import jax
import jax.numpy as jnp
from jax import lax
from jax.sharding import PartitionSpec as P

B = 256
REACH = 2


def padded(x, sides, width):
    for axis, dim in sides:
        devices, length = (lax.axis_size(axis), x.shape[dim])
        up = [(i, (i + 1) % devices) for i in range(devices - 1)]
        down = [(j, i) for i, j in up]
        last = lax.slice_in_dim(x, length - width, length, axis=dim)
        initial = lax.slice_in_dim(x, 0, width, axis=dim)
        before = lax.ppermute(last, axis, up)
        after = lax.ppermute(initial, axis, down)
        x = jnp.concatenate([before, x, after], axis=dim)
    return x


def partner(value, axis, stride):
    mask = 2**stride
    pairs = [(source, source ^ mask) for source in range(lax.axis_size(axis))]
    return lax.ppermute(value, axis, pairs)


def per_device(vectors, near_tiles, near_cols, left_one, right_one, left_two, right_two):
    vector_count = vectors.shape[1]
    levels = lax.axis_size("rows").bit_length() - 1
    extended = padded(vectors, (("rows", 0),), REACH * B)
    blocks = extended.reshape(extended.shape[0] // B, B, vector_count)
    picked = blocks[near_cols]
    near_part = jnp.einsum("tkab,tkbn->tan", near_tiles, picked, preferred_element_type=jnp.float32)
    near_part = near_part.reshape(-1, vector_count)
    proj_one = jnp.einsum("mr,mn->rn", right_one, vectors, preferred_element_type=jnp.float32)
    proj_two = jnp.einsum("mr,mn->rn", right_two, vectors, preferred_element_type=jnp.float32)
    acc_one = proj_one
    for level_bit in range(levels - 1):
        acc_one = acc_one + partner(acc_one.astype(jnp.bfloat16), "rows", level_bit).astype(
            acc_one.dtype
        )
    far_one = partner(acc_one.astype(jnp.bfloat16), "rows", levels - 1).astype(acc_one.dtype)
    acc_two = proj_two
    for level_bit in range(levels - 2):
        acc_two = acc_two + partner(acc_two.astype(jnp.bfloat16), "rows", level_bit).astype(
            acc_two.dtype
        )
    far_two = partner(acc_two.astype(jnp.bfloat16), "rows", levels - 2).astype(acc_two.dtype)
    coeff_one = far_one.astype(jnp.bfloat16)
    second_coefficient = far_two.astype(jnp.bfloat16)
    lowrank = lax.psum_scatter(
        (
            jnp.dot(left_one, coeff_one, preferred_element_type=jnp.float32)
            + jnp.dot(left_two, second_coefficient, preferred_element_type=jnp.float32)
        ).astype(jnp.bfloat16),
        "cols",
        scatter_dimension=0,
        tiled=True,
    ).astype(jnp.float32)
    return (near_part + lowrank).astype(jnp.bfloat16)


def solution(mesh):
    placed = (
        P("rows", None),
        P(("rows", "cols"), None, None, None),
        P(("rows", "cols"), None),
        P("rows", "cols"),
        P("rows", "cols"),
        P("rows", "cols"),
        P("rows", "cols"),
    )
    return jax.shard_map(
        per_device, mesh=mesh, in_specs=placed, out_specs=P(("rows", "cols"), None), check_vma=False
    )
```

profile of v0, /device:TPU:46, one launch (start us, length us, event | category | flops | bytes accessed | tf_op | source)
XLA Modules:
  0.0 221.9 jit_solution(2199624511265237562)
XLA Ops:
  6.5 5.1 %fusion.8 = (bf16[128,1024]{1,0:T(8,128)(2,1)S(1)}, f32[128,1024]{1,0:T(8,128)S(1)}) fusion(bf16[4096,128]{1,0:T(8,128)(2,1)} %param.11, bf16[4096,1024]{1,0:T(8,128)(2,1)} %param.7), kind=kOutput, calls=%fused_computation.21 | convolution fusion | flops 1073872896 | bytes 10223616 | tf_op jit(solution)/shard_map/mr,mn->rn/dot_general | solution.py:37
  11.7 0.5 collective-permute-start.2
  12.2 0.8 copy-done.2
  13.0 1.3 fusion.7
  14.4 0.9 collective-permute-start.7
  15.2 5.7 %collective-permute-done.2 = bf16[128,1024]{1,0:T(8,128)(2,1)S(1)} collective-permute-done((bf16[128,1024]{1,0:T(8,128)(2,1)S(1)}, bf16[128,1024]{1,0:T(8,128)(2,1)S(1)}, u32[]{:S(2)}, u32[]{:S(2)}) %collective-permute-start.2) | collective-permute-done | bytes 262176 | tf_op jit(solution)/shard_map/ppermute | solution.py:26
  21.2 4.2 %collective-permute-done.7 = bf16[128,1024]{1,0:T(8,128)(2,1)S(1)} collective-permute-done((bf16[128,1024]{1,0:T(8,128)(2,1)S(1)}, bf16[128,1024]{1,0:T(8,128)(2,1)S(1)}, u32[]{:S(2)}, u32[]{:S(2)}) %collective-permute-start.7) | collective-permute-done | bytes 262176 | tf_op jit(solution)/shard_map/ppermute | solution.py:26
  25.7 2.1 collective-permute-done.3
  27.9 3.0 %collective-permute-start.4 = (bf16[128,1024]{1,0:T(8,128)(2,1)S(1)}, bf16[128,1024]{1,0:T(8,128)(2,1)S(1)}, u32[]{:S(2)}, u32[]{:S(2)}) collective-permute-start(bf16[128,1024]{1,0:T(8,128)(2,1)S(1)} %fusion.5), channel_id=1, source_target_pairs={{0,16},{4,20},{8,24},{12,28},{16,0},{20,4},{24,8},{28,12},{32,48},... | collective-permute-start | bytes 786440 | tf_op jit(solution)/shard_map/ppermute | solution.py:26
  30.9 3.9 %collective-permute-done.8 = bf16[128,1024]{1,0:T(8,128)(2,1)S(1)} collective-permute-done((bf16[128,1024]{1,0:T(8,128)(2,1)S(1)}, bf16[128,1024]{1,0:T(8,128)(2,1)S(1)}, u32[]{:S(2)}, u32[]{:S(2)}) %collective-permute-start.8) | collective-permute-done | bytes 262176 | tf_op jit(solution)/shard_map/ppermute | solution.py:26
  34.9 3.1 %collective-permute-start.9 = (bf16[128,1024]{1,0:T(8,128)(2,1)S(1)}, bf16[128,1024]{1,0:T(8,128)(2,1)S(1)}, u32[]{:S(2)}, u32[]{:S(2)}) collective-permute-start(bf16[128,1024]{1,0:T(8,128)(2,1)S(1)} %fusion.4), channel_id=1, source_target_pairs={{0,16},{4,20},{8,24},{12,28},{16,0},{20,4},{24,8},{28,12},{32,48},... | collective-permute-start | bytes 786440 | tf_op jit(solution)/shard_map/ppermute | solution.py:26
  37.9 3.8 %collective-permute-done.4 = bf16[128,1024]{1,0:T(8,128)(2,1)S(1)} collective-permute-done((bf16[128,1024]{1,0:T(8,128)(2,1)S(1)}, bf16[128,1024]{1,0:T(8,128)(2,1)S(1)}, u32[]{:S(2)}, u32[]{:S(2)}) %collective-permute-start.4) | collective-permute-done | bytes 262176 | tf_op jit(solution)/shard_map/ppermute | solution.py:26
  41.9 0.9 collective-permute-start.5
  42.8 2.9 %collective-permute-done.9 = bf16[128,1024]{1,0:T(8,128)(2,1)S(1)} collective-permute-done((bf16[128,1024]{1,0:T(8,128)(2,1)S(1)}, bf16[128,1024]{1,0:T(8,128)(2,1)S(1)}, u32[]{:S(2)}, u32[]{:S(2)}) %collective-permute-start.9) | collective-permute-done | bytes 262176 | tf_op jit(solution)/shard_map/ppermute | solution.py:26
  45.8 0.9 collective-permute-start.10
  46.7 3.0 %collective-permute-done.5 = bf16[128,1024]{1,0:T(8,128)(2,1)S(1)} collective-permute-done((bf16[128,1024]{1,0:T(8,128)(2,1)S(1)}, bf16[128,1024]{1,0:T(8,128)(2,1)S(1)}, u32[]{:S(2)}, u32[]{:S(2)}) %collective-permute-start.5) | collective-permute-done | bytes 262176 | tf_op jit(solution)/shard_map/ppermute | solution.py:26
  49.8 0.2 add_convert_fusion.3
  50.0 1.5 collective-permute-start.6
  51.5 3.9 %collective-permute-done.10 = bf16[128,1024]{1,0:T(8,128)(2,1)S(1)} collective-permute-done((bf16[128,1024]{1,0:T(8,128)(2,1)S(1)}, bf16[128,1024]{1,0:T(8,128)(2,1)S(1)}, u32[]{:S(2)}, u32[]{:S(2)}) %collective-permute-start.10) | collective-permute-done | bytes 262176 | tf_op jit(solution)/shard_map/ppermute | solution.py:26
  55.4 8.1 %fusion.9 = f32[1024,4096]{1,0:T(8,128)} fusion(bf16[128,1024]{1,0:T(8,128)(2,1)S(1)} %collective-permute-done.10, bf16[4096,128]{1,0:T(8,128)(2,1)S(1)} %copy-done), kind=kOutput, calls=%fused_computation.22 | convolution fusion | flops 1073741824 | bytes 18087936 | tf_op jit(solution)/shard_map/dot_general | solution.py:56
  63.5 11.5 %fusion = bf16[4096,1024]{0,1:T(8,128)(2,1)} fusion(f32[1024,4096]{1,0:T(8,128)} %fusion.9, bf16[128,1024]{1,0:T(8,128)(2,1)S(1)} %collective-permute-done.6, bf16[4096,128]{1,0:T(8,128)(2,1)S(1)} %copy-done.4), kind=kOutput, calls=%fused_computation.3 | convolution fusion | flops 1082130432 | bytes 26476544 | tf_op jit(solution)/shard_map/dot_general | solution.py:55
  75.1 2.7 %fusion.6 = (bf16[512,1024]{1,0:T(8,128)(2,1)S(1)}, bf16[512,1024]{1,0:T(8,128)(2,1)}) fusion(bf16[4096,1024]{1,0:T(8,128)(2,1)} %param.7), kind=kLoop, calls=%fused_computation.19 | loop fusion | bytes 4194304 | tf_op jit(solution)/shard_map/slice | solution.py:15
  77.7 2.4 %collective-permute-start.1 = (bf16[512,1024]{1,0:T(8,128)(2,1)}, bf16[512,1024]{1,0:T(8,128)(2,1)S(1)}, u32[]{:S(2)}, u32[]{:S(2)}) collective-permute-start(bf16[512,1024]{1,0:T(8,128)(2,1)} %get-tuple-element.6), channel_id=1, source_target_pairs={{4,0},{8,4},{12,8},{16,12},{20,16},{24,20},{28,24},{32,28},{36,32}... | collective-permute-start | bytes 3145736 | tf_op jit(solution)/shard_map/ppermute | solution.py:18
  80.1 4.6 %collective-permute-start = (bf16[512,1024]{1,0:T(8,128)(2,1)S(1)}, bf16[512,1024]{1,0:T(8,128)(2,1)S(1)}, u32[]{:S(2)}, u32[]{:S(2)}) collective-permute-start(bf16[512,1024]{1,0:T(8,128)(2,1)S(1)} %get-tuple-element.5), channel_id=1, source_target_pairs={{0,4},{4,8},{8,12},{12,16},{16,20},{20,24},{24,28},{28,32},{32,36}... | collective-permute-start | bytes 3145736 | tf_op jit(solution)/shard_map/ppermute | solution.py:17
  84.8 22.7 %collective-permute-done.1 = bf16[512,1024]{1,0:T(8,128)(2,1)S(1)} collective-permute-done((bf16[512,1024]{1,0:T(8,128)(2,1)}, bf16[512,1024]{1,0:T(8,128)(2,1)S(1)}, u32[]{:S(2)}, u32[]{:S(2)}) %collective-permute-start.1) | collective-permute-done | bytes 1048608 | tf_op jit(solution)/shard_map/ppermute | solution.py:18
  107.5 43.8 %collective-permute-done = bf16[512,1024]{1,0:T(8,128)(2,1)S(1)} collective-permute-done((bf16[512,1024]{1,0:T(8,128)(2,1)S(1)}, bf16[512,1024]{1,0:T(8,128)(2,1)S(1)}, u32[]{:S(2)}, u32[]{:S(2)}) %collective-permute-start) | collective-permute-done | bytes 1048608 | tf_op jit(solution)/shard_map/ppermute | solution.py:17
  151.3 16.9 %pad_maximum_fusion = bf16[5120,1024]{1,0:T(8,128)(2,1)} fusion(bf16[512,1024]{1,0:T(8,128)(2,1)S(1)} %collective-permute-done.1, bf16[4096,1024]{1,0:T(8,128)(2,1)} %param.7, bf16[512,1024]{1,0:T(8,128)(2,1)S(1)} %collective-permute-done), kind=kLoop, calls=%fused_computation.2 | loop fusion | flops 31457280 | bytes 20971520 | tf_op jit(solution)/shard_map/concatenate | solution.py:19
  168.2 16.4 %gather_fusion = bf16[64,256,1024]{2,1,0:T(8,128)(2,1)} fusion(bf16[20,256,1024]{2,1,0:T(8,128)(2,1)} %bitcast.20, s32[1024]{0:T(1024)S(1)} %pad_clamp_fusion), kind=kCustom, calls=%fused_computation | custom fusion | bytes 67109120 | tf_op jit(solution)/shard_map/gather | solution.py:34
  184.6 18.8 %fusion.10 = f32[4,1024,256,1]{1,2,3,0:T(8,128)} fusion(bf16[4,16,256,256]{3,2,1,0:T(8,128)(2,1)} %param.8, bf16[4,16,256,1024]{3,2,1,0:T(8,128)(2,1)} %bitcast.21), kind=kOutput, calls=%fused_computation.23 | convolution fusion | flops 8589934592 | bytes 46137344 | tf_op jit(solution)/shard_map/tkab,tkbn->tan/dot_general | solution.py:35
  203.4 5.4 %copy.8 = f32[1024,1024]{0,1:T(8,128)} copy(f32[1024,1024]{1,0:T(8,128)} %bitcast.22) | data formatting | bytes 8388608 | tf_op jit(solution)/shard_map/reshape | solution.py:36
  208.9 3.6 %add_convert_fusion.1 = bf16[1024,1024]{0,1:T(8,128)(2,1)S(1)} fusion(f32[1024,1024]{0,1:T(8,128)} %copy.8, bf16[1024,1024]{0,1:T(8,128)(2,1)} %reduce-scatter.2.cloned.1.call-done), kind=kLoop, calls=%fused_computation.4 | loop fusion | flops 3145728 | bytes 8388608 | tf_op jit(solution)/shard_map/convert_element_type | solution.py:62
  212.5 2.6 %copy.9 = bf16[1024,1024]{1,0:T(8,128)(2,1)} copy(bf16[1024,1024]{0,1:T(8,128)(2,1)S(1)} %add_convert_fusion.1) | data formatting | bytes 4194304 | tf_op jit(solution)/shard_map/convert_element_type | solution.py:62
  (26 shorter events, 1.2 us)
Async XLA Ops:
  6.5 48.9 %copy-start = (bf16[4096,128]{1,0:T(8,128)(2,1)S(1)}, bf16[4096,128]{1,0:T(8,128)(2,1)}, u32[]{:S(2)}) copy-start(bf16[4096,128]{1,0:T(8,128)(2,1)} %param.12) | copy-start | bytes 3145732
  6.5 5.7 %copy-start.3 = (bf16[4096,128]{1,0:T(8,128)(2,1)S(1)}, bf16[4096,128]{1,0:T(8,128)(2,1)}, u32[]{:S(2)}) copy-start(bf16[4096,128]{1,0:T(8,128)(2,1)} %param.13) | copy-start | bytes 3145732
  6.5 202.3 %reduce-scatter.2.cloned.1.call-start = ((), (), s32[]{:S(2)}) async-start(), calls=%async_computation.1 | async-start | bytes 10485760 | tf_op jit(solution)/shard_map/reduce_scatter | solution.py:53
  6.5 6.5 %copy-start.2 = (bf16[4096,1024]{1,0:T(8,128)(2,1)S(1)}, bf16[4096,1024]{1,0:T(8,128)(2,1)}, u32[]{:S(2)}) copy-start(bf16[4096,1024]{1,0:T(8,128)(2,1)} %param.7) | copy-start | bytes 25165828
  11.7 9.3 %collective-permute-start.2 = (bf16[128,1024]{1,0:T(8,128)(2,1)S(1)}, bf16[128,1024]{1,0:T(8,128)(2,1)S(1)}, u32[]{:S(2)}, u32[]{:S(2)}) collective-permute-start(bf16[128,1024]{1,0:T(8,128)(2,1)S(1)} %get-tuple-element.9), channel_id=1, source_target_pairs={{0,4},{4,0},{8,12},{12,8},{16,20},{20,16},{24,28},{28,24},{32,36},... | collective-permute-start | bytes 786440 | tf_op jit(solution)/shard_map/ppermute | solution.py:26
  14.4 11.0 %collective-permute-start.7 = (bf16[128,1024]{1,0:T(8,128)(2,1)S(1)}, bf16[128,1024]{1,0:T(8,128)(2,1)S(1)}, u32[]{:S(2)}, u32[]{:S(2)}) collective-permute-start(bf16[128,1024]{1,0:T(8,128)(2,1)S(1)} %get-tuple-element.7), channel_id=1, source_target_pairs={{0,4},{4,0},{8,12},{12,8},{16,20},{20,16},{24,28},{28,24},{32,36},... | collective-permute-start | bytes 786440 | tf_op jit(solution)/shard_map/ppermute | solution.py:26
  21.0 6.8 %collective-permute-start.3 = (bf16[128,1024]{1,0:T(8,128)(2,1)S(1)}, bf16[128,1024]{1,0:T(8,128)(2,1)S(1)}, u32[]{:S(2)}, u32[]{:S(2)}) collective-permute-start(bf16[128,1024]{1,0:T(8,128)(2,1)S(1)} %fusion.1), channel_id=1, source_target_pairs={{0,8},{4,12},{8,0},{12,4},{16,24},{20,28},{24,16},{28,20},{32,40},... | collective-permute-start | bytes 786440 | tf_op jit(solution)/shard_map/ppermute | solution.py:26
  25.5 9.3 %collective-permute-start.8 = (bf16[128,1024]{1,0:T(8,128)(2,1)S(1)}, bf16[128,1024]{1,0:T(8,128)(2,1)S(1)}, u32[]{:S(2)}, u32[]{:S(2)}) collective-permute-start(bf16[128,1024]{1,0:T(8,128)(2,1)S(1)} %fusion.3), channel_id=1, source_target_pairs={{0,8},{4,12},{8,0},{12,4},{16,24},{20,28},{24,16},{28,20},{32,40},... | collective-permute-start | bytes 786440 | tf_op jit(solution)/shard_map/ppermute | solution.py:26
  27.9 13.9 %collective-permute-start.4 = (bf16[128,1024]{1,0:T(8,128)(2,1)S(1)}, bf16[128,1024]{1,0:T(8,128)(2,1)S(1)}, u32[]{:S(2)}, u32[]{:S(2)}) collective-permute-start(bf16[128,1024]{1,0:T(8,128)(2,1)S(1)} %fusion.5), channel_id=1, source_target_pairs={{0,16},{4,20},{8,24},{12,28},{16,0},{20,4},{24,8},{28,12},{32,48},... | collective-permute-start | bytes 786440 | tf_op jit(solution)/shard_map/ppermute | solution.py:26
  34.9 10.8 %collective-permute-start.9 = (bf16[128,1024]{1,0:T(8,128)(2,1)S(1)}, bf16[128,1024]{1,0:T(8,128)(2,1)S(1)}, u32[]{:S(2)}, u32[]{:S(2)}) collective-permute-start(bf16[128,1024]{1,0:T(8,128)(2,1)S(1)} %fusion.4), channel_id=1, source_target_pairs={{0,16},{4,20},{8,24},{12,28},{16,0},{20,4},{24,8},{28,12},{32,48},... | collective-permute-start | bytes 786440 | tf_op jit(solution)/shard_map/ppermute | solution.py:26
  41.9 7.9 %collective-permute-start.5 = (bf16[128,1024]{1,0:T(8,128)(2,1)S(1)}, bf16[128,1024]{1,0:T(8,128)(2,1)S(1)}, u32[]{:S(2)}, u32[]{:S(2)}) collective-permute-start(bf16[128,1024]{1,0:T(8,128)(2,1)S(1)} %fusion.2), channel_id=1, source_target_pairs={{0,32},{4,36},{8,40},{12,44},{16,48},{20,52},{24,56},{28,60},{32,0... | collective-permute-start | bytes 786440 | tf_op jit(solution)/shard_map/ppermute | solution.py:26
  45.8 9.6 %collective-permute-start.10 = (bf16[128,1024]{1,0:T(8,128)(2,1)S(1)}, bf16[128,1024]{1,0:T(8,128)(2,1)S(1)}, u32[]{:S(2)}, u32[]{:S(2)}) collective-permute-start(bf16[128,1024]{1,0:T(8,128)(2,1)S(1)} %add_convert_fusion.2), channel_id=1, source_target_pairs={{0,32},{4,36},{8,40},{12,44},{16,48},{20,52},{24,56},{28,60},{32,0... | collective-permute-start | bytes 786440 | tf_op jit(solution)/shard_map/ppermute | solution.py:26
  50.0 13.5 %copy-start.4 = (bf16[4096,128]{1,0:T(8,128)(2,1)S(1)}, bf16[4096,128]{1,0:T(8,128)(2,1)}, u32[]{:S(2)}) copy-start(bf16[4096,128]{1,0:T(8,128)(2,1)} %param.10) | copy-start | bytes 3145732
  50.0 13.5 %collective-permute-start.6 = (bf16[128,1024]{1,0:T(8,128)(2,1)S(1)}, bf16[128,1024]{1,0:T(8,128)(2,1)S(1)}, u32[]{:S(2)}, u32[]{:S(2)}) collective-permute-start(bf16[128,1024]{1,0:T(8,128)(2,1)S(1)} %add_convert_fusion.3), channel_id=1, source_target_pairs={{0,64},{4,68},{8,72},{12,76},{16,80},{20,84},{24,88},{28,92},{32,9... | collective-permute-start | bytes 786440 | tf_op jit(solution)/shard_map/ppermute | solution.py:26
  75.0 9.6 %copy-start.5 = (s32[4,16]{1,0:T(4,128)S(1)}, s32[4,16]{1,0:T(4,128)}, u32[]{:S(2)}) copy-start(s32[4,16]{1,0:T(4,128)} %param.9) | copy-start | bytes 772
  77.7 29.8 %collective-permute-start.1 = (bf16[512,1024]{1,0:T(8,128)(2,1)}, bf16[512,1024]{1,0:T(8,128)(2,1)S(1)}, u32[]{:S(2)}, u32[]{:S(2)}) collective-permute-start(bf16[512,1024]{1,0:T(8,128)(2,1)} %get-tuple-element.6), channel_id=1, source_target_pairs={{4,0},{8,4},{12,8},{16,12},{20,16},{24,20},{28,24},{32,28},{36,32}... | collective-permute-start | bytes 3145736 | tf_op jit(solution)/shard_map/ppermute | solution.py:18
  80.1 71.2 %collective-permute-start = (bf16[512,1024]{1,0:T(8,128)(2,1)S(1)}, bf16[512,1024]{1,0:T(8,128)(2,1)S(1)}, u32[]{:S(2)}, u32[]{:S(2)}) collective-permute-start(bf16[512,1024]{1,0:T(8,128)(2,1)S(1)} %get-tuple-element.5), channel_id=1, source_target_pairs={{0,4},{4,8},{8,12},{12,16},{16,20},{20,24},{24,28},{28,32},{32,36}... | collective-permute-start | bytes 3145736 | tf_op jit(solution)/shard_map/ppermute | solution.py:17
  203.4 11.7 %copy-start.1 = (bf16[4096,128]{1,0:T(8,128)(2,1)S(1)}, bf16[4096,128]{1,0:T(8,128)(2,1)}, u32[]{:S(2)}) copy-start(bf16[4096,128]{1,0:T(8,128)(2,1)} %param.12) | copy-start | bytes 3145732
Sparse Core Ops, SparseCore 0:
  75.2 96.8 reduce-scatter.1
where the time goes:
time: 222 us
  waiting for transfers between devices  96 us (43%)
  matrix products  44.9 us (20%)
  local copies, waits for them, and re-layouts  28 us (13%)
  other arithmetic  21.4 us (10%)
  starting transfers between devices  18.1 us (8%)
  between operations  13.5 us (6%)
    ppermute x1, waiting for transfers between devices, padded(): before = lax.ppermute(last, axis, up)  43.8 us
    ppermute x9, waiting for transfers between devices, partner(): return lax.ppermute(value, axis, pairs)  29.5 us
    ppermute x1, waiting for transfers between devices, padded(): after = lax.ppermute(initial, axis, down)  22.7 us
    dot_general x1, matrix products, per_device(): jnp.einsum('tkab,tkbn->tan', near_tiles, picked, preferred_element_type=j...  18.8 us
    concatenate x1, other arithmetic, padded(): x = jnp.concatenate([before, x, after], axis=dim)  16.9 us
    gather x1, local copies, waits for them, and re-layouts, per_device(): picked = blocks[near_cols]  16.4 us
    dot_general x1, matrix products, per_device(): jnp.dot(left_one, coeff_one, preferred_element_type=jnp.float32)  11.5 us
    ppermute x9, starting transfers between devices, partner(): return lax.ppermute(value, axis, pairs)  11.2 us
  transfers between devices with their start and end apart: 12, of which 10 were waited for; matrix products, arithmetic and copies ran while one was open for 32% of the time, Pallas kernels for 0%

commit v1 on v0

v1 whole, which is shorter than its diff:
```python
import jax
import jax.numpy as jnp
from jax import lax
from jax.experimental import pallas as pl
from jax.experimental.pallas import tpu as pltpu
from jax.sharding import PartitionSpec as P

B = 256
REACH = 2
NNZ = 16
TILES = 4
OWN = 16
WINDOW = OWN + 2 * REACH
M = OWN * B
N = 1024
HALO = REACH * B
QUARTER = HALO // 4
ROWS = TILES * B
RB = 128
HALF = ROWS // 2
BF = jnp.bfloat16
F32 = jnp.float32


def kernel(
    inv,
    vec,
    near,
    left_one,
    left_two,
    right_one,
    right_two,
    out,
    win,
    nt,
    dense,
    rt,
    pacc,
    part,
    zin,
    ysend,
    yin,
    keep,
    xsend,
    xin,
    coeff,
    left,
    relay,
    acc,
    vec_sem,
    loc_sem,
    hop_s,
    hop_r,
    fwd_s,
    fwd_r,
    swap_s,
    swap_r,
    halo_s,
    halo_r,
    share_s,
    share_r,
    z_s,
    z_r,
    y_s,
    y_r,
    x_s,
    x_r,
    g_s,
    g_r,
    ring_s,
    ring_r,
    core_s,
    core_r,
):
    lefts = (left_one, left_two)
    r = lax.axis_index("rows")
    c = lax.axis_index("cols")
    x = r // 8
    z = (r // 2) % 4
    yl = r % 2
    yh = c // 2
    k = c % 2
    flip = r + 1 - 2 * yl
    oh = 1 - yh
    ok = 1 - k
    highs = (yh, oh)

    def dev(row, high, core):
        return (row, high * 2 + core)

    def at_z(zz):
        return x * 8 + zz * 2 + yl

    def at_x(xx):
        return xx * 8 + z * 2 + yl

    zp = (z + 1) % 4
    zm = (z + 3) % 4
    zo = (z + 2) % 4
    x1 = x + 1 - 2 * (x % 2)
    x2 = (x + 2) % 4
    x3 = 3 - x
    xpar = x % 2
    up = (r + 1) % 32
    down = (r + 31) % 32
    other = dev(r, yh, ok)

    def rcopy(src, dst, send, recv, target):
        return pltpu.make_async_remote_copy(
            src_ref=src,
            dst_ref=dst,
            send_sem=send,
            recv_sem=recv,
            device_id=target,
            device_id_type=pl.DeviceIdType.MESH,
        )

    steps = 4
    rows = M // steps
    vec_in = [
        pltpu.make_async_copy(
            vec.at[pl.ds(i * rows, rows)], win.at[pl.ds(HALO + i * rows, rows)], vec_sem.at[i]
        )
        for i in range(steps)
    ]
    right_in = [
        pltpu.make_async_copy(right_one, rt.at[:, pl.ds(0, RB)], loc_sem.at[0]),
        pltpu.make_async_copy(right_two, rt.at[:, pl.ds(RB, RB)], loc_sem.at[1]),
    ]
    near_in = pltpu.make_async_copy(near, nt.at[:, pl.ds(0, NNZ)], loc_sem.at[2])
    left_in = [
        pltpu.make_async_copy(
            lefts[l].at[pl.ds(c * ROWS, ROWS)], left.at[k, l, yh], loc_sem.at[3 + l]
        )
        for l in range(2)
    ]
    for copy in right_in + vec_in + [near_in] + left_in:
        copy.start()

    barrier = pltpu.get_barrier_semaphore()
    partners = [
        dev(up, yh, k),
        dev(up, oh, k),
        dev(down, yh, k),
        dev(down, oh, k),
        dev(flip, yh, ok),
        dev(flip, oh, ok),
        dev(r, oh, k),
        other,
        dev(at_z(zp), yh, k),
        dev(at_z(zm), yh, k),
        dev(at_z(zo), yh, k),
        dev(at_x(x1), yh, k),
        dev(at_x(x2), yh, k),
        dev(at_x(x3), yh, k),
    ]
    for partner in partners:
        pl.semaphore_signal(
            barrier, inc=1, device_id=partner, device_id_type=pl.DeviceIdType.MESH
        )
    pl.semaphore_wait(barrier, len(partners))

    hops = {}
    forwards = {}
    for p in range(2):
        for core in range(2):
            for l in range(2):
                hops[p, core, l] = rcopy(
                    lefts[l].at[pl.ds((oh * 2 + core) * ROWS + p * HALF, HALF)],
                    relay.at[p, core, l],
                    hop_s.at[p, core, l],
                    hop_r.at[p, core, l],
                    dev(flip, highs[p], k),
                )
                forwards[p, core, l] = rcopy(
                    relay.at[p, core, l],
                    left.at[k, l, highs[p], pl.ds(p * HALF, HALF)],
                    fwd_s.at[p, core, l],
                    fwd_r.at[p, k, l],
                    dev(flip, highs[1 - p], core),
                )
    arrivals = {
        (p, core, l): rcopy(
            relay.at[p, core, l],
            left.at[core, l, oh, pl.ds(p * HALF, HALF)],
            fwd_s.at[p, core, l],
            fwd_r.at[p, core, l],
            dev(flip, highs[p], core),
        )
        for p in range(2)
        for core in range(2)
        for l in range(2)
    }
    swaps = [
        rcopy(
            lefts[l].at[pl.ds((yh * 2 + ok) * ROWS, ROWS)],
            left.at[k, l, yh],
            swap_s.at[l],
            swap_r.at[l],
            other,
        )
        for l in range(2)
    ]
    for core in range(2):
        for l in range(2):
            for p in range(2):
                hops[p, core, l].start()
    for copy in swaps:
        copy.start()

    for copy in right_in:
        copy.wait()
    for i in range(steps):
        vec_in[i].wait()
        term = lax.dot_general(
            rt[pl.ds(i * rows, rows), :],
            win[pl.ds(HALO + i * rows, rows), :],
            (((0,), (0,)), ((), ())),
            preferred_element_type=F32,
        )
        if i == 0:
            pacc[...] = term
        else:
            pacc[...] += term
    for l in range(2):
        for zz in range(4):
            part[zz, l] = pacc[pl.ds(l * RB + zz * 32, 32), :].astype(BF)
    targets = (zp, zo, zm)
    z_out = [
        rcopy(
            part.at[targets[j]],
            zin.at[z],
            z_s.at[j],
            z_r.at[j],
            dev(at_z(targets[j]), yh, k),
        )
        for j in range(3)
    ]
    for j in (1, 0, 2):
        z_out[j].start()

    nt[:, NNZ] = jnp.zeros((TILES, B, B), BF)
    near_in.wait()

    def assemble(w, carry):
        for t in range(TILES):
            dense[pl.ds(t * B, B), pl.ds(pl.multiple_of(w * B, B), B)] = nt[t, inv[t, w]]
        return carry

    lax.fori_loop(0, WINDOW, assemble, 0)

    def near_part(first, depth, initial=False):
        def columns(i, carry):
            cols = pl.ds(pl.multiple_of(i * B, B), B)
            term = jnp.dot(
                dense[:, pl.ds(first, depth)],
                win[pl.ds(first, depth), cols],
                preferred_element_type=F32,
            )
            if initial:
                acc[:, cols] = term
            else:
                acc[:, cols] += term
            return carry

        lax.fori_loop(0, N // B, columns, 0)

    near_part(HALO, 1024, True)

    for copy in z_out:
        copy.wait_recv()
    for l in range(2):
        base = pl.multiple_of(l * RB + z * 32, 32)
        total = pacc[pl.ds(base, 32), :]
        for j in range(1, 4):
            total = total + zin[(z + j) % 4, l].astype(F32)
        pacc[pl.ds(base, 32), :] = total
        keep[l] = pacc[pl.ds(pl.multiple_of(base + yl * 16, 16), 16), :]
        ysend[l] = pacc[pl.ds(pl.multiple_of(base + (1 - yl) * 16, 16), 16), :].astype(BF)
    y_out = rcopy(ysend, yin, y_s.at[0], y_r.at[0], dev(flip, yh, k))
    y_out.start()

    halos = {}
    shares = {}
    for d in range(2):
        for p in range(2):
            quarter = (2 * p + k) * QUARTER
            source = quarter + (M - HALO if d == 0 else 0)
            place = win.at[pl.ds(quarter + (0 if d == 0 else HALO + M), QUARTER)]
            halos[d, p] = rcopy(
                vec.at[pl.ds(source, QUARTER)],
                place,
                halo_s.at[d, p],
                halo_r.at[d, p],
                dev(up if d == 0 else down, highs[p], k),
            )
            shares[d, p] = rcopy(place, place, share_s.at[d, p], share_r.at[d, p], other)
    sends = (r < 31, r > 0)
    gets = (r > 0, r < 31)

    def halo_start(d):
        @pl.when(sends[d])
        def _():
            for p in range(2):
                halos[d, p].start()

    def halo_share(d):
        @pl.when(gets[d])
        def _():
            for p in range(2):
                halos[d, p].wait_recv()
                shares[d, p].start()

        @pl.when(jnp.logical_not(gets[d]))
        def _():
            win[pl.ds(0 if d == 0 else HALO + M, HALO), :] = jnp.zeros((HALO, N), BF)

    def halo_wait(d):
        @pl.when(gets[d])
        def _():
            for p in range(2):
                shares[d, p].wait()

        @pl.when(sends[d])
        def _():
            for p in range(2):
                halos[d, p].wait_send()

    halo_start(0)
    near_part(HALO + 1024, 1024)

    y_out.wait()
    for l in range(2):
        xsend[l] = (keep[l] + yin[l].astype(F32)).astype(BF)
    x_out = [
        rcopy(
            xsend.at[1], coeff.at[k, 1, yh, z, yl], x_s.at[0], x_r.at[0], dev(at_x(x1), yh, k)
        ),
        rcopy(xsend.at[0], xin.at[xpar], x_s.at[1], x_r.at[1], dev(at_x(x2), yh, k)),
        rcopy(xsend.at[0], xin.at[xpar], x_s.at[2], x_r.at[2], dev(at_x(x3), yh, k)),
    ]
    for copy in x_out:
        copy.start()
    near_part(HALO + 2048, 1024)
    for copy in x_out:
        copy.wait()
    coeff[k, 0, yh, z, yl] = (xin[0].astype(F32) + xin[1].astype(F32)).astype(BF)

    mine = coeff.at[k, :, yh, z, yl]
    g_out = [
        rcopy(mine, mine, g_s.at[i], g_r.at[i], target)
        for i, target in enumerate((dev(flip, yh, k), dev(flip, oh, k), dev(r, oh, k)))
    ]
    for i in (2, 0, 1):
        g_out[i].start()
    halo_start(1)
    for core in range(2):
        for l in range(2):
            for p in range(2):
                hops[p, core, l].wait_recv()
                forwards[p, core, l].start()
    near_part(HALO + 3072, 1024)
    for copy in g_out:
        copy.wait()

    def at(zz):
        return coeff.at[k, :, :, zz]

    def level(l, zz):
        return coeff.at[k, l, :, zz]

    ring = [
        rcopy(at(z), at(z), ring_s.at[0], ring_r.at[0], dev(at_z(zp), yh, k)),
        rcopy(at(z), at(z), ring_s.at[1], ring_r.at[1], dev(at_z(zm), yh, k)),
        rcopy(level(0, zm), level(0, zm), ring_s.at[2], ring_r.at[2], dev(at_z(zp), yh, k)),
        rcopy(level(1, zp), level(1, zp), ring_s.at[3], ring_r.at[3], dev(at_z(zm), yh, k)),
    ]
    cores = [
        rcopy(part_, part_, core_s.at[i], core_r.at[i], other)
        for i, part_ in enumerate((at(z), at(zm), at(zp), level(0, zo), level(1, zo)))
    ]
    ring[0].start()
    ring[1].start()
    cores[0].start()
    halo_share(0)
    for i in range(2):
        ring[i].wait_recv()
        ring[i + 2].start()
        cores[i + 1].start()
    halo_wait(0)
    near_part(0, HALO)
    for i in range(2):
        ring[i + 2].wait_recv()
        cores[i + 3].start()
    halo_share(1)
    halo_wait(1)
    near_part(HALO + M, HALO)

    for copy in cores + swaps:
        copy.wait()
    for copy in left_in:
        copy.wait()
    for p in range(2):
        for core in range(2):
            for l in range(2):
                arrivals[p, core, l].wait_recv()
        here = pl.ds(p * HALF, HALF)

        def columns(i, carry):
            cols = pl.ds(pl.multiple_of(i * B, B), B)
            basis = jnp.concatenate(
                [left[a, b, h, here, :] for a in range(2) for b in range(2) for h in range(2)],
                axis=1,
            )
            far = jnp.dot(
                basis, coeff[..., cols].reshape(8 * RB, B), preferred_element_type=F32
            )
            out[here, cols] = (acc[here, cols] + far).astype(out.dtype)
            return carry

        lax.fori_loop(0, N // B, columns, 0)

    for copy in list(hops.values()) + list(forwards.values()) + z_out + ring:
        copy.wait_send()


def per_device(vectors, near_tiles, near_cols, left_one, right_one, left_two, right_two):
    named = near_cols[:, :, None] == jnp.arange(WINDOW, dtype=jnp.int32)
    order = jnp.arange(NNZ, dtype=jnp.int32)[None, :, None] - NNZ
    inv = NNZ + jnp.sum(jnp.where(named, order, 0), axis=1).astype(jnp.int32)
    dma = pltpu.SemaphoreType.DMA
    hbm = pl.BlockSpec(memory_space=pltpu.HBM)
    return pl.pallas_call(
        kernel,
        out_shape=jax.ShapeDtypeStruct((ROWS, N), BF),
        in_specs=[pl.BlockSpec(memory_space=pltpu.SMEM)] + [hbm] * 6,
        out_specs=pl.BlockSpec(memory_space=pltpu.VMEM),
        scratch_shapes=[
            pltpu.VMEM((WINDOW * B, N), BF),
            pltpu.VMEM((TILES, NNZ + 1, B, B), BF),
            pltpu.VMEM((ROWS, WINDOW * B), BF),
            pltpu.VMEM((M, 2 * RB), BF),
            pltpu.VMEM((2 * RB, N), F32),
            pltpu.VMEM((4, 2, 32, N), BF),
            pltpu.VMEM((4, 2, 32, N), BF),
            pltpu.VMEM((2, 16, N), BF),
            pltpu.VMEM((2, 16, N), BF),
            pltpu.VMEM((2, 16, N), F32),
            pltpu.VMEM((2, 16, N), BF),
            pltpu.VMEM((2, 16, N), BF),
            pltpu.VMEM((2, 2, 2, 4, 2, 16, N), BF),
            pltpu.VMEM((2, 2, 2, ROWS, RB), BF),
            pltpu.VMEM((2, 2, 2, HALF, RB), BF),
            pltpu.VMEM((ROWS, N), F32),
            dma((4,)),
            dma((5,)),
            dma((2, 2, 2)),
            dma((2, 2, 2)),
            dma((2, 2, 2)),
            dma((2, 2, 2)),
            dma((2,)),
            dma((2,)),
            dma((2, 2)),
            dma((2, 2)),
            dma((2, 2)),
            dma((2, 2)),
            dma((3,)),
            dma((3,)),
            dma((1,)),
            dma((1,)),
            dma((3,)),
            dma((3,)),
            dma((3,)),
            dma((3,)),
            dma((4,)),
            dma((4,)),
            dma((5,)),
            dma((5,)),
        ],
        compiler_params=pltpu.CompilerParams(
            collective_id=0, has_side_effects=True, vmem_limit_bytes=56 * 1024 * 1024
        ),
    )(inv, vectors, near_tiles, left_one, left_two, right_one, right_two)


def solution(mesh):
    placed = (
        P("rows", None),
        P(("rows", "cols"), None, None, None),
        P(("rows", "cols"), None),
        P("rows", "cols"),
        P("rows", "cols"),
        P("rows", "cols"),
        P("rows", "cols"),
    )
    return jax.shard_map(
        per_device, mesh=mesh, in_specs=placed, out_specs=P(("rows", "cols"), None), check_vma=False
    )
```

time: 222 us -> 68.1 us (0.31)
  the two profiles are of different devices: /device:TPU:46 before, /device:TPU:41 now
where the time goes in v1:
time: 68.1 us; the launch traced here: 67.9 us
  Pallas kernels  63.5 us (93%)
  local copies, waits for them, and re-layouts  3.08 us (5%)
  other arithmetic  1.36 us (2%)
    pallas_call x1, Pallas kernels, per_device(): pl.pallas_call(kernel, out_shape=jax.ShapeDtypeStruct((ROWS, N), BF), in_...  63.5 us
    unnamed x1, local copies, waits for them, and re-layouts  3.08 us

profile of v1, /device:TPU:41, one launch (start us, length us, event | category | flops | bytes accessed | tf_op | source)
XLA Modules:
  0.0 67.9 jit_solution(10341347912042797650)
XLA Ops:
  0.0 0.8 %select_reduce_fusion = s32[4,20]{1,0:T(4,128)S(1)} fusion(s32[16]{0:T(128)S(1)} %iota_add_fusion, s32[4,16]{1,0:T(4,128)} %param.9), kind=kLoop, calls=%fused_computation | loop fusion | flops 3760 | bytes 640 | tf_op jit(solution)/shard_map/reduce_sum | solution.py:430
  0.8 0.6 broadcast_add_fusion.inv
  1.4 63.5 %shard_map.73 = bf16[1024,1024]{1,0:T(8,128)(2,1)} custom-call(s32[4,20]{1,0:T(4,128)} %broadcast_add_fusion.inv, bf16[4096,1024]{1,0:T(8,128)(2,1)} %vec.1, bf16[4,16,256,256]{3,2,1,0:T(8,128)(2,1)} %near.1, bf16[4096,128]{1,0:T(8,128)(2,1)} %left_one.1, bf16[4096,128]{1,0:T(8,128)(2,1)} %left_two.1, bf16[4096,128]{1,0:T(8,128)(2,1)} %right_one.1, ...), custom_call_target="tpu_custom_call" | custom-call | tf_op jit(solution)/shard_map/pallas_call | solution.py:433
  64.9 3.1 %copy.9 = bf16[1024,1024]{1,0:T(8,128)(2,1)} copy(bf16[1024,1024]{1,0:T(8,128)(2,1)} %shard_map.73) | data formatting | bytes 4194304
  (1 shorter events, 0.0 us)

commit v2 on v1

v2 whole, which is shorter than its diff:
```python
import jax
import jax.numpy as jnp
from jax import lax
from jax.experimental import pallas as pl
from jax.experimental.pallas import tpu as pltpu
from jax.sharding import PartitionSpec as P

B = 256
REACH = 2
NNZ = 16
TILES = 4
OWN = 16
WINDOW = OWN + 2 * REACH
M = OWN * B
N = 1024
HALO = REACH * B
QUARTER = HALO // 4
ROWS = TILES * B
RB = 128
HALF = ROWS // 2
PIECE = HALF // 2
STEPS = 8
EARLY = 4
FIRST = 5
PLAN = (2, 4, 4, 4)
BF = jnp.bfloat16
F32 = jnp.float32


def kernel(
    cols,
    vec,
    near,
    left_one,
    left_two,
    right_one,
    right_two,
    out,
    win,
    nt,
    dense,
    rt,
    pacc,
    part,
    zin,
    zrelay,
    ysend,
    yin,
    keep,
    xsend,
    xin,
    coeff,
    left,
    relay,
    far_rows,
    acc,
    vec_sem,
    right_sem,
    loc_sem,
    hop_s,
    hop_r,
    fwd_s,
    fwd_r,
    swap_s,
    swap_r,
    far_s,
    far_r,
    near_s,
    near_r,
    halo_s,
    halo_r,
    share_s,
    share_r,
    z_s,
    z_r,
    y_s,
    y_r,
    x_s,
    x_r,
    g_s,
    g_r,
    ring_s,
    ring_r,
    core_s,
    core_r,
):
    lefts = (left_one, left_two)
    rights = (right_one, right_two)
    r = lax.axis_index("rows")
    c = lax.axis_index("cols")
    x = r // 8
    z = (r // 2) % 4
    yl = r % 2
    yh = c // 2
    k = c % 2
    flip = r + 1 - 2 * yl
    oh = 1 - yh
    ok = 1 - k
    highs = (yh, oh)

    def dev(row, high, core):
        return (row, high * 2 + core)

    def at_z(zz):
        return x * 8 + zz * 2 + yl

    def at_x(xx):
        return xx * 8 + z * 2 + yl

    zp = (z + 1) % 4
    zm = (z + 3) % 4
    zo = (z + 2) % 4
    x1 = x + 1 - 2 * (x % 2)
    x2 = (x + 2) % 4
    x3 = 3 - x
    xpar = x % 2
    other = dev(r, yh, ok)

    def rcopy(src, dst, send, recv, target):
        return pltpu.make_async_remote_copy(
            src_ref=src,
            dst_ref=dst,
            send_sem=send,
            recv_sem=recv,
            device_id=target,
            device_id_type=pl.DeviceIdType.MESH,
        )

    barrier = pltpu.get_barrier_semaphore()
    partners = [
        dev(flip, yh, k),
        dev(flip, oh, k),
        dev(flip, yh, ok),
        dev(flip, oh, ok),
        dev(r, oh, k),
        other,
        dev(at_z(zp), yh, k),
        dev(at_z(zm), yh, k),
        dev(at_x(x1), yh, k),
        dev(at_x(x2), yh, k),
        dev(at_x(x3), yh, k),
        dev((r + 2) % 32, yh, k),
        dev((r + 30) % 32, yh, k),
    ]
    for partner in partners:
        pl.semaphore_signal(
            barrier, inc=1, device_id=partner, device_id_type=pl.DeviceIdType.MESH
        )

    rows = M // STEPS
    vec_in = [
        pltpu.make_async_copy(
            vec.at[pl.ds(i * rows, rows)], win.at[pl.ds(HALO + i * rows, rows)], vec_sem.at[i]
        )
        for i in range(STEPS)
    ]
    right_in = [
        [
            pltpu.make_async_copy(
                rights[l].at[pl.ds(i * rows, rows)],
                rt.at[pl.ds(i * rows, rows), pl.ds(l * RB, RB)],
                right_sem.at[i],
            )
            for l in range(2)
        ]
        for i in range(STEPS)
    ]
    near_in = pltpu.make_async_copy(near, nt.at[:, pl.ds(0, NNZ)], loc_sem.at[2])
    left_in = [
        pltpu.make_async_copy(
            lefts[l].at[pl.ds(c * ROWS, ROWS)], left.at[k, l, yh], loc_sem.at[l]
        )
        for l in range(2)
    ]
    for i in range(STEPS):
        for copy in right_in[i] + [vec_in[i]]:
            copy.start()

    pieces = [(s, core, l) for s in range(2) for core in range(2) for l in range(2)]
    hops = {}
    forwards = {}
    for s, core, l in pieces:
        for p in range(2):
            off = s * HALF + p * PIECE
            hops[p, s, core, l] = rcopy(
                lefts[l].at[pl.ds((oh * 2 + core) * ROWS + off, PIECE)],
                relay.at[p, s, core, l],
                hop_s.at[p, s],
                hop_r.at[p, s],
                dev(flip, highs[p], k),
            )
            forwards[p, s, core, l] = rcopy(
                relay.at[p, s, core, l],
                left.at[k, l, highs[p], pl.ds(off, PIECE)],
                fwd_s.at[p, s],
                fwd_r.at[s, k],
                dev(flip, highs[1 - p], core),
            )
    hop_all = {
        (p, s): rcopy(
            relay.at[p, s], relay.at[p, s], hop_s.at[p, s], hop_r.at[p, s], dev(flip, highs[p], k)
        )
        for p in range(2)
        for s in range(2)
    }
    fwd_all = {
        (p, s): rcopy(
            relay.at[p, s], relay.at[p, s], fwd_s.at[p, s], fwd_r.at[s, k], dev(flip, highs[p], k)
        )
        for p in range(2)
        for s in range(2)
    }

    def arrival(s, core):
        here = left.at[core, :, oh, pl.ds(s * HALF, HALF)]
        return rcopy(here, here, fwd_s.at[0, s], fwd_r.at[s, core], dev(flip, yh, k))

    swaps = [
        rcopy(
            lefts[l].at[pl.ds((yh * 2 + ok) * ROWS, ROWS)],
            left.at[k, l, yh],
            swap_s.at[l],
            swap_r.at[l],
            other,
        )
        for l in range(2)
    ]

    def hop_start(some):
        for s, core, l in some:
            for p in range(2):
                hops[p, s, core, l].start()

    def forward_start(s):
        for p in range(2):
            hop_all[p, s].wait_recv()
        for core in range(2):
            for l in range(2):
                for p in range(2):
                    forwards[p, s, core, l].start()

    def project(low, high):
        for i in range(low, high):
            taken = rt.at[pl.ds(i * rows, rows)]
            pltpu.make_async_copy(taken, taken, right_sem.at[i]).wait()
            vec_in[i].wait()
            term = lax.dot_general(
                rt[pl.ds(i * rows, rows), :],
                win[pl.ds(HALO + i * rows, rows), :],
                (((0,), (0,)), ((), ())),
                preferred_element_type=F32,
            )
            if i == 0:
                pacc[...] = term
            else:
                pacc[...] += term

    project(0, EARLY)
    pl.semaphore_wait(barrier, len(partners))
    hop_start(pieces[:FIRST])
    near_in.start()
    project(EARLY, STEPS)
    for l in range(2):
        for zz in range(4):
            part[zz, l] = pacc[pl.ds(l * RB + zz * 32, 32), :].astype(BF)
    ways = (dev(at_z(zp), yh, k), dev(at_z(zm), yh, k))
    nexts = (zp, zm)
    lasts = (zm, zp)
    halves = (pl.ds(0, 16), pl.ds(16, 16))
    z_hop = []
    z_out = []
    z_fwd = []
    for d in range(2):
        z_hop.append(
            rcopy(part.at[zo, :, halves[d]], zrelay.at[d], z_s.at[0, d], z_r.at[0, d], ways[d])
        )
        z_out.append(rcopy(part.at[nexts[d]], zin.at[z], z_s.at[1, d], z_r.at[1, d], ways[d]))
        z_fwd.append(
            rcopy(
                zrelay.at[d], zin.at[lasts[d], :, halves[d]], z_s.at[2, d], z_r.at[2, d], ways[d]
            )
        )
    for copy in z_hop + z_out:
        copy.start()

    near_base = pl.multiple_of((1 - yl) * (HALO + M), HALO)
    far_base = pl.multiple_of(yl * (HALO + M), HALO)
    edge = jnp.logical_and(r > 0, r < 31)
    relays = jnp.logical_and(flip > 0, flip < 31)
    far_out = rcopy(
        vec.at[pl.ds(yl * (M - HALO) + (2 * yh + k) * QUARTER, QUARTER)],
        far_rows,
        far_s.at[0],
        far_r.at[0],
        dev((r + 30 + 4 * yl) % 32, yh, k),
    )
    near_halo = []
    far_halo = []
    near_share = []
    far_share = []
    for p in range(2):
        quarter = (2 * p + k) * QUARTER
        for i in range(2):
            piece = quarter + i * (QUARTER // 2)
            near_halo.append(
                rcopy(
                    vec.at[pl.ds((1 - yl) * (M - HALO) + piece, QUARTER // 2)],
                    win.at[pl.ds(far_base + piece, QUARTER // 2)],
                    near_s.at[p, i],
                    near_r.at[p, i],
                    dev(flip, highs[p], k),
                )
            )
        place = win.at[pl.ds(near_base + quarter, QUARTER)]
        near_share.append(rcopy(place, place, share_s.at[0, p], share_r.at[0, p], other))
        far_halo.append(
            rcopy(
                far_rows,
                win.at[pl.ds(near_base + (2 * yh + k) * QUARTER, QUARTER)],
                halo_s.at[p],
                halo_r.at[p],
                dev(flip, highs[p], k),
            )
        )
        place = win.at[pl.ds(far_base + (2 * highs[p] + k) * QUARTER, QUARTER)]
        far_share.append(rcopy(place, place, share_s.at[1, p], share_r.at[1, p], other))

    for copy in swaps + left_in:
        copy.start()

    nt[:, NNZ] = jnp.zeros((TILES, B, B), BF)
    near_in.wait()
    for d in range(2):
        z_hop[d].wait_recv()
        z_fwd[d].start()

    @pl.when(edge)
    def _():
        far_out.start()

    def assemble(w, carry):
        for t in range(TILES):
            place = jnp.int32(NNZ)
            for j in range(NNZ):
                place = jnp.where(cols[t, j] == w, j, place)
            dense[pl.ds(t * B, B), pl.ds(pl.multiple_of(w * B, B), B)] = nt[t, place]
        return carry

    lax.fori_loop(0, WINDOW, assemble, 0)

    def near_part(first, depth, low, high, initial=False):
        def columns(i, carry):
            here = pl.ds(pl.multiple_of(i * B, B), B)
            term = jnp.dot(
                dense[:, pl.ds(first, depth)],
                win[pl.ds(first, depth), here],
                preferred_element_type=F32,
            )
            if initial:
                acc[:, here] = term
            else:
                acc[:, here] += term
            return carry

        lax.fori_loop(low, high, columns, 0)

    done = [0]

    def advance(count):
        while count > 0:
            slab, low = divmod(done[0], 4)
            high = min(4, low + count)
            near_part(HALO + slab * 1024, 1024, low, high, slab == 0)
            done[0] += high - low
            count -= high - low

    advance(PLAN[0])

    for copy in z_out + z_fwd:
        copy.wait_recv()
    for l in range(2):
        base = pl.multiple_of(l * RB + z * 32, 32)
        total = pacc[pl.ds(base, 32), :]
        for j in range(1, 4):
            total = total + zin[(z + j) % 4, l].astype(F32)
        pacc[pl.ds(base, 32), :] = total
        keep[l] = pacc[pl.ds(pl.multiple_of(base + yl * 16, 16), 16), :]
        ysend[l] = pacc[pl.ds(pl.multiple_of(base + (1 - yl) * 16, 16), 16), :].astype(BF)
    y_out = rcopy(ysend, yin, y_s.at[0], y_r.at[0], dev(flip, yh, k))
    y_out.start()
    hop_start(pieces[FIRST:])
    advance(PLAN[1])

    y_out.wait()
    for l in range(2):
        xsend[l] = (keep[l] + yin[l].astype(F32)).astype(BF)
    x_out = [
        rcopy(
            xsend.at[1], coeff.at[k, 1, yh, z, yl], x_s.at[0], x_r.at[0], dev(at_x(x1), yh, k)
        ),
        rcopy(xsend.at[0], xin.at[xpar], x_s.at[1], x_r.at[1], dev(at_x(x2), yh, k)),
        rcopy(xsend.at[0], xin.at[xpar], x_s.at[2], x_r.at[2], dev(at_x(x3), yh, k)),
    ]
    for i in (1, 2, 0):
        x_out[i].start()
    near_halo[0].start()
    near_halo[2].start()
    advance(PLAN[2])
    for copy in x_out:
        copy.wait_recv()
    coeff[k, 0, yh, z, yl] = (xin[0].astype(F32) + xin[1].astype(F32)).astype(BF)

    mine = coeff.at[k, :, yh, z, yl]
    g_out = [
        rcopy(mine, mine, g_s.at[i], g_r.at[i], target)
        for i, target in enumerate((dev(flip, yh, k), dev(flip, oh, k), dev(r, oh, k)))
    ]
    for i in (2, 0, 1):
        g_out[i].start()
    near_halo[1].start()
    near_halo[3].start()

    @pl.when(relays)
    def _():
        far_out.wait_recv()
        for copy in far_halo:
            copy.start()

    forward_start(0)
    advance(PLAN[3])
    for copy in g_out:
        copy.wait_recv()

    def level(l, zz):
        return coeff.at[k, l, :, zz]

    def ring_copy(l, zz, d, i):
        return rcopy(level(l, zz), level(l, zz), ring_s.at[d, i], ring_r.at[d, i], ways[d])

    ring = [
        [ring_copy(d, z, d, 0), ring_copy(1 - d, z, d, 1), ring_copy(d, lasts[d], d, 2)]
        for d in range(2)
    ]

    def core_start(l, zz):
        rcopy(level(l, zz), level(l, zz), core_s.at[0], core_r.at[0], other).start()

    core_out = rcopy(coeff.at[k], coeff.at[k], core_s.at[0], core_r.at[0], other)
    for i in range(2):
        for d in range(2):
            ring[d][i].start()
    for l in range(2):
        core_start(l, z)
    forward_start(1)
    advance(16 - done[0])
    for d in range(2):
        ring[d][0].wait_recv()
        ring[d][2].start()
        core_start(d, lasts[d])
    for copy in near_halo:
        copy.wait_recv()
    for copy in near_share:
        copy.start()
    for d in range(2):
        ring[d][1].wait_recv()
        core_start(1 - d, lasts[d])
    for copy in near_share:
        copy.wait_recv()
    near_part(near_base, HALO, 0, 4)

    @pl.when(edge)
    def _():
        for copy in far_halo:
            copy.wait_recv()
        for copy in far_share:
            copy.start()

    for d in range(2):
        ring[d][2].wait_recv()
        core_start(d, zo)

    @pl.when(edge)
    def _():
        for copy in far_share:
            copy.wait()

    @pl.when(jnp.logical_not(edge))
    def _():
        win[pl.ds(far_base, HALO), :] = jnp.zeros((HALO, N), BF)

    near_part(far_base, HALO, 0, 4)

    def far_part(chips, low, count, target):
        blocks = [(a, l, h) for a in range(2) for l in range(2) for h in chips]

        def columns(i, carry):
            here = pl.ds(pl.multiple_of(i * B, B), B)
            basis = jnp.concatenate([left[a, l, h, pl.ds(low, count)] for a, l, h in blocks], axis=1)
            weights = jnp.concatenate(
                [coeff[a, l, h, :, :, :, here].reshape(RB, B) for a, l, h in blocks], axis=0
            )
            term = jnp.dot(basis, weights, preferred_element_type=F32)
            total = acc[pl.ds(low, count), here] + term
            target[pl.ds(low, count), here] = total.astype(target.dtype)
            return carry

        lax.fori_loop(0, N // B, columns, 0)

    for copy in left_in:
        copy.wait()
    for copy in swaps:
        copy.wait_recv()
    core_out.wait_recv()
    far_part((yh,), HALF, HALF, acc)
    for core in range(2):
        arrival(0, core).wait_recv()
    far_part((0, 1), 0, HALF, out)
    for core in range(2):
        arrival(1, core).wait_recv()
    far_part((oh,), HALF, HALF, out)

    for copy in (
        list(hop_all.values())
        + list(fwd_all.values())
        + z_hop
        + z_out
        + z_fwd
        + x_out
        + g_out
        + ring[0]
        + ring[1]
        + [core_out]
        + swaps
        + near_halo
        + near_share
    ):
        copy.wait_send()

    @pl.when(edge)
    def _():
        far_out.wait_send()

    @pl.when(relays)
    def _():
        for copy in far_halo:
            copy.wait_send()


def per_device(vectors, near_tiles, near_cols, left_one, right_one, left_two, right_two):
    hbm = pl.BlockSpec(memory_space=pltpu.HBM)
    counts = [
        (STEPS,),
        (STEPS,),
        (3,),
        (2, 2),
        (2, 2),
        (2, 2),
        (2, 2),
        (2,),
        (2,),
        (1,),
        (1,),
        (2, 2),
        (2, 2),
        (2,),
        (2,),
        (2, 2),
        (2, 2),
        (3, 2),
        (3, 2),
        (1,),
        (1,),
        (3,),
        (3,),
        (3,),
        (3,),
        (2, 3),
        (2, 3),
        (1,),
        (1,),
    ]
    return pl.pallas_call(
        kernel,
        out_shape=pltpu.VMEM((ROWS, N), BF),
        in_specs=[pl.BlockSpec(memory_space=pltpu.SMEM)] + [hbm] * 6,
        out_specs=pl.BlockSpec(memory_space=pltpu.VMEM),
        scratch_shapes=[
            pltpu.VMEM((WINDOW * B, N), BF),
            pltpu.VMEM((TILES, NNZ + 1, B, B), BF),
            pltpu.VMEM((ROWS, WINDOW * B), BF),
            pltpu.VMEM((M, 2 * RB), BF),
            pltpu.VMEM((2 * RB, N), F32),
            pltpu.VMEM((4, 2, 32, N), BF),
            pltpu.VMEM((4, 2, 32, N), BF),
            pltpu.VMEM((2, 2, 16, N), BF),
            pltpu.VMEM((2, 16, N), BF),
            pltpu.VMEM((2, 16, N), BF),
            pltpu.VMEM((2, 16, N), F32),
            pltpu.VMEM((2, 16, N), BF),
            pltpu.VMEM((2, 16, N), BF),
            pltpu.VMEM((2, 2, 2, 4, 2, 16, N), BF),
            pltpu.VMEM((2, 2, 2, ROWS, RB), BF),
            pltpu.VMEM((2, 2, 2, 2, PIECE, RB), BF),
            pltpu.VMEM((QUARTER, N), BF),
            pltpu.VMEM((ROWS, N), F32),
        ]
        + [pltpu.SemaphoreType.DMA(shape) for shape in counts],
        compiler_params=pltpu.CompilerParams(
            collective_id=0, has_side_effects=True, vmem_limit_bytes=54 * 1024 * 1024
        ),
    )(near_cols, vectors, near_tiles, left_one, left_two, right_one, right_two)


def solution(mesh):
    placed = (
        P("rows", None),
        P(("rows", "cols"), None, None, None),
        P(("rows", "cols"), None),
        P("rows", "cols"),
        P("rows", "cols"),
        P("rows", "cols"),
        P("rows", "cols"),
    )
    return jax.shard_map(
        per_device, mesh=mesh, in_specs=placed, out_specs=P(("rows", "cols"), None), check_vma=False
    )
```

time: 68.1 us -> 58.1 us (0.85)
  the two profiles are of different devices: /device:TPU:41 before, /device:TPU:3 now
where the time goes in v2:
time: 58.1 us; the launch traced here: 58 us
  Pallas kernels  56.7 us (98%)
  local copies, waits for them, and re-layouts  1.32 us (2%)
    pallas_call x1, Pallas kernels, per_device(): pl.pallas_call(kernel, out_shape=pltpu.VMEM((ROWS, N), BF), in_specs=[pl....  56.7 us
    unnamed x1, local copies, waits for them, and re-layouts  1.32 us

profile of v2, /device:TPU:3, one launch (start us, length us, event | category | flops | bytes accessed | tf_op | source)
XLA Modules:
  0.0 58.0 jit_solution(17897975442660544986)
XLA Ops:
  0.0 56.7 %shard_map.73 = bf16[1024,1024]{1,0:T(8,128)(2,1)S(1)} custom-call(s32[4,16]{1,0:T(4,128)} %cols.1, bf16[4096,1024]{1,0:T(8,128)(2,1)} %vec.1, bf16[4,16,256,256]{3,2,1,0:T(8,128)(2,1)} %near.1, bf16[4096,128]{1,0:T(8,128)(2,1)} %left_one.1, bf16[4096,128]{1,0:T(8,128)(2,1)} %left_two.1, bf16[4096,128]{1,0:T(8,128)(2,1)} %right_one.1, ...), custom_call_target="tpu_custom_call" | custom-call | tf_op jit(solution)/shard_map/pallas_call | solution.py:582
  56.7 1.3 %copy.9 = bf16[1024,1024]{1,0:T(8,128)(2,1)} copy(bf16[1024,1024]{1,0:T(8,128)(2,1)S(1)} %shard_map.73) | data formatting | bytes 4194304

commit v3 on v2

--- a/solution.py
+++ b/solution.py
@@ -21,8 +21,7 @@
 PIECE = HALF // 2
 STEPS = 8
 EARLY = 4
-FIRST = 5
-PLAN = (2, 4, 4, 4)
+PLAN = (2, 6, 5)
 BF = jnp.bfloat16
 F32 = jnp.float32
 
@@ -44,9 +43,6 @@
     part,
     zin,
     zrelay,
-    ysend,
-    yin,
-    keep,
     xsend,
     xin,
     coeff,
@@ -73,8 +69,6 @@
     share_r,
     z_s,
     z_r,
-    y_s,
-    y_r,
     x_s,
     x_r,
     g_s,
@@ -139,6 +133,9 @@
         dev(at_x(x1), yh, k),
         dev(at_x(x2), yh, k),
         dev(at_x(x3), yh, k),
+        dev(at_x(x1) + flip - r, yh, k),
+        dev(at_x(x2) + flip - r, yh, k),
+        dev(at_x(x3) + flip - r, yh, k),
         dev((r + 2) % 32, yh, k),
         dev((r + 30) % 32, yh, k),
     ]
@@ -257,7 +254,7 @@
 
     project(0, EARLY)
     pl.semaphore_wait(barrier, len(partners))
-    hop_start(pieces[:FIRST])
+    hop_start(pieces)
     near_in.start()
     project(EARLY, STEPS)
     for l in range(2):
@@ -334,10 +331,6 @@
         z_hop[d].wait_recv()
         z_fwd[d].start()
 
-    @pl.when(edge)
-    def _():
-        far_out.start()
-
     def assemble(w, carry):
         for t in range(TILES):
             place = jnp.int32(NNZ)
@@ -383,32 +376,32 @@
         total = pacc[pl.ds(base, 32), :]
         for j in range(1, 4):
             total = total + zin[(z + j) % 4, l].astype(F32)
-        pacc[pl.ds(base, 32), :] = total
-        keep[l] = pacc[pl.ds(pl.multiple_of(base + yl * 16, 16), 16), :]
-        ysend[l] = pacc[pl.ds(pl.multiple_of(base + (1 - yl) * 16, 16), 16), :].astype(BF)
-    y_out = rcopy(ysend, yin, y_s.at[0], y_r.at[0], dev(flip, yh, k))
-    y_out.start()
-    hop_start(pieces[FIRST:])
+        for low in range(2):
+            xsend[l, low] = total[low * 16 : low * 16 + 16].astype(BF)
+
+    for low in (1 - yl, yl):
+        for l, plane, slot in ((0, x2, xpar), (0, x3, xpar), (1, x1, 2)):
+            rcopy(
+                xsend.at[l, low],
+                xin.at[slot, yl],
+                x_s.at[0],
+                x_r.at[0],
+                dev(plane * 8 + z * 2 + low, yh, k),
+            ).start()
+    x_all = rcopy(xin, xin, x_s.at[0], x_r.at[0], dev(at_x(x1), yh, k))
+    for copy in near_halo:
+        copy.start()
+
+    @pl.when(edge)
+    def _():
+        far_out.start()
+
     advance(PLAN[1])
-
-    y_out.wait()
-    for l in range(2):
-        xsend[l] = (keep[l] + yin[l].astype(F32)).astype(BF)
-    x_out = [
-        rcopy(
-            xsend.at[1], coeff.at[k, 1, yh, z, yl], x_s.at[0], x_r.at[0], dev(at_x(x1), yh, k)
-        ),
-        rcopy(xsend.at[0], xin.at[xpar], x_s.at[1], x_r.at[1], dev(at_x(x2), yh, k)),
-        rcopy(xsend.at[0], xin.at[xpar], x_s.at[2], x_r.at[2], dev(at_x(x3), yh, k)),
-    ]
-    for i in (1, 2, 0):
-        x_out[i].start()
-    near_halo[0].start()
-    near_halo[2].start()
-    advance(PLAN[2])
-    for copy in x_out:
-        copy.wait_recv()
-    coeff[k, 0, yh, z, yl] = (xin[0].astype(F32) + xin[1].astype(F32)).astype(BF)
+    x_all.wait_recv()
+    first = xin[0, 0].astype(F32) + xin[0, 1].astype(F32)
+    first = first + (xin[1, 0].astype(F32) + xin[1, 1].astype(F32))
+    coeff[k, 0, yh, z, yl] = first.astype(BF)
+    coeff[k, 1, yh, z, yl] = (xin[2, 0].astype(F32) + xin[2, 1].astype(F32)).astype(BF)
 
     mine = coeff.at[k, :, yh, z, yl]
     g_out = [
@@ -417,8 +410,6 @@
     ]
     for i in (2, 0, 1):
         g_out[i].start()
-    near_halo[1].start()
-    near_halo[3].start()
 
     @pl.when(relays)
     def _():
@@ -427,7 +418,7 @@
             copy.start()
 
     forward_start(0)
-    advance(PLAN[3])
+    advance(PLAN[2])
     for copy in g_out:
         copy.wait_recv()
 
@@ -453,20 +444,20 @@
         core_start(l, z)
     forward_start(1)
     advance(16 - done[0])
-    for d in range(2):
-        ring[d][0].wait_recv()
-        ring[d][2].start()
-        core_start(d, lasts[d])
     for copy in near_halo:
         copy.wait_recv()
     for copy in near_share:
         copy.start()
     for d in range(2):
-        ring[d][1].wait_recv()
-        core_start(1 - d, lasts[d])
+        ring[d][0].wait_recv()
+        ring[d][2].start()
+        core_start(d, lasts[d])
     for copy in near_share:
         copy.wait_recv()
     near_part(near_base, HALO, 0, 4)
+    for d in range(2):
+        ring[d][1].wait_recv()
+        core_start(1 - d, lasts[d])
 
     @pl.when(edge)
     def _():
@@ -525,7 +516,7 @@
         + z_hop
         + z_out
         + z_fwd
-        + x_out
+        + [x_all]
         + g_out
         + ring[0]
         + ring[1]
@@ -570,8 +561,6 @@
         (3, 2),
         (1,),
         (1,),
-        (3,),
-        (3,),
         (3,),
         (3,),
         (2, 3),
@@ -593,11 +582,8 @@
             pltpu.VMEM((4, 2, 32, N), BF),
             pltpu.VMEM((4, 2, 32, N), BF),
             pltpu.VMEM((2, 2, 16, N), BF),
-            pltpu.VMEM((2, 16, N), BF),
-            pltpu.VMEM((2, 16, N), BF),
-            pltpu.VMEM((2, 16, N), F32),
-            pltpu.VMEM((2, 16, N), BF),
-            pltpu.VMEM((2, 16, N), BF),
+            pltpu.VMEM((2, 2, 16, N), BF),
+            pltpu.VMEM((3, 2, 16, N), BF),
             pltpu.VMEM((2, 2, 2, 4, 2, 16, N), BF),
             pltpu.VMEM((2, 2, 2, ROWS, RB), BF),
             pltpu.VMEM((2, 2, 2, 2, PIECE, RB), BF),

time: 58.1 us -> 50.7 us (0.87)
  Pallas kernels: 56.7 us -> 49 us
    pallas_call x1, Pallas kernels: 56.7 us -> 49 us  [per_device(): pl.pallas_call(kernel, out_shape=pltpu.VMEM((ROWS, N), BF), in_specs=[pl....]
where the time goes in v3:
time: 50.7 us; the launch traced here: 50.3 us
  Pallas kernels  49 us (97%)
  local copies, waits for them, and re-layouts  1.32 us (3%)
    pallas_call x1, Pallas kernels, per_device(): pl.pallas_call(kernel, out_shape=pltpu.VMEM((ROWS, N), BF), in_specs=[pl....  49 us
    unnamed x1, local copies, waits for them, and re-layouts  1.32 us

profile of v3, /device:TPU:3, one launch (start us, length us, event | category | flops | bytes accessed | tf_op | source)
XLA Modules:
  0.0 50.3 jit_solution(7027443009588536468)
XLA Ops:
  0.0 49.0 %shard_map.73 = bf16[1024,1024]{1,0:T(8,128)(2,1)S(1)} custom-call(s32[4,16]{1,0:T(4,128)} %cols.1, bf16[4096,1024]{1,0:T(8,128)(2,1)} %vec.1, bf16[4,16,256,256]{3,2,1,0:T(8,128)(2,1)} %near.1, bf16[4096,128]{1,0:T(8,128)(2,1)} %left_one.1, bf16[4096,128]{1,0:T(8,128)(2,1)} %left_two.1, bf16[4096,128]{1,0:T(8,128)(2,1)} %right_one.1, ...), custom_call_target="tpu_custom_call" | custom-call | tf_op jit(solution)/shard_map/pallas_call | solution.py:571
  49.0 1.3 %copy.9 = bf16[1024,1024]{1,0:T(8,128)(2,1)} copy(bf16[1024,1024]{1,0:T(8,128)(2,1)S(1)} %shard_map.73) | data formatting | bytes 4194304

commit v4 on v3

--- a/solution.py
+++ b/solution.py
@@ -18,10 +18,11 @@
 ROWS = TILES * B
 RB = 128
 HALF = ROWS // 2
-PIECE = HALF // 2
+BLOCKS = ((0, 768), (768, 256))
+SPLIT = ((80, 32), (112, 32))
 STEPS = 8
-EARLY = 4
-PLAN = (2, 6, 5)
+EARLY = 1
+PLAN = (5, 5, 3)
 BF = jnp.bfloat16
 F32 = jnp.float32
 
@@ -126,7 +127,6 @@
         dev(flip, oh, k),
         dev(flip, yh, ok),
         dev(flip, oh, ok),
-        dev(r, oh, k),
         other,
         dev(at_z(zp), yh, k),
         dev(at_z(zm), yh, k),
@@ -176,40 +176,46 @@
     pieces = [(s, core, l) for s in range(2) for core in range(2) for l in range(2)]
     hops = {}
     forwards = {}
+    def slot(p, s, core=slice(None), l=slice(None)):
+        return relay.at[p, core, l, pl.ds(BLOCKS[s][0] // 2, BLOCKS[s][1] // 2)]
+
+    def part_of(p, s):
+        return BLOCKS[s][0] + p * (BLOCKS[s][1] // 2), BLOCKS[s][1] // 2
+
     for s, core, l in pieces:
         for p in range(2):
-            off = s * HALF + p * PIECE
+            off, size = part_of(p, s)
             hops[p, s, core, l] = rcopy(
-                lefts[l].at[pl.ds((oh * 2 + core) * ROWS + off, PIECE)],
-                relay.at[p, s, core, l],
+                lefts[l].at[pl.ds((oh * 2 + core) * ROWS + off, size)],
+                slot(p, s, core, l),
                 hop_s.at[p, s],
                 hop_r.at[p, s],
                 dev(flip, highs[p], k),
             )
             forwards[p, s, core, l] = rcopy(
-                relay.at[p, s, core, l],
-                left.at[k, l, highs[p], pl.ds(off, PIECE)],
+                slot(p, s, core, l),
+                left.at[k, l, highs[p], pl.ds(off, size)],
                 fwd_s.at[p, s],
                 fwd_r.at[s, k],
                 dev(flip, highs[1 - p], core),
             )
     hop_all = {
         (p, s): rcopy(
-            relay.at[p, s], relay.at[p, s], hop_s.at[p, s], hop_r.at[p, s], dev(flip, highs[p], k)
+            slot(p, s), slot(p, s), hop_s.at[p, s], hop_r.at[p, s], dev(flip, highs[p], k)
         )
         for p in range(2)
         for s in range(2)
     }
     fwd_all = {
         (p, s): rcopy(
-            relay.at[p, s], relay.at[p, s], fwd_s.at[p, s], fwd_r.at[s, k], dev(flip, highs[p], k)
+            slot(p, s), slot(p, s), fwd_s.at[p, s], fwd_r.at[s, k], dev(flip, highs[p], k)
         )
         for p in range(2)
         for s in range(2)
     }
 
     def arrival(s, core):
-        here = left.at[core, :, oh, pl.ds(s * HALF, HALF)]
+        here = left.at[core, :, oh, pl.ds(*BLOCKS[s])]
         return rcopy(here, here, fwd_s.at[0, s], fwd_r.at[s, core], dev(flip, yh, k))
 
     swaps = [
@@ -296,19 +302,19 @@
     near_share = []
     far_share = []
     for p in range(2):
-        quarter = (2 * p + k) * QUARTER
+        half = k * (HALO // 2) + p * sum(SPLIT[0])
         for i in range(2):
-            piece = quarter + i * (QUARTER // 2)
+            mine = half + i * SPLIT[p][0]
             near_halo.append(
                 rcopy(
-                    vec.at[pl.ds((1 - yl) * (M - HALO) + piece, QUARTER // 2)],
-                    win.at[pl.ds(far_base + piece, QUARTER // 2)],
+                    vec.at[pl.ds((1 - yl) * (M - HALO) + mine, SPLIT[p][i])],
+                    win.at[pl.ds(far_base + mine, SPLIT[p][i])],
                     near_s.at[p, i],
                     near_r.at[p, i],
                     dev(flip, highs[p], k),
                 )
             )
-        place = win.at[pl.ds(near_base + quarter, QUARTER)]
+        place = win.at[pl.ds(near_base + half, sum(SPLIT[p]))]
         near_share.append(rcopy(place, place, share_s.at[0, p], share_r.at[0, p], other))
         far_halo.append(
             rcopy(
@@ -327,9 +333,6 @@
 
     nt[:, NNZ] = jnp.zeros((TILES, B, B), BF)
     near_in.wait()
-    for d in range(2):
-        z_hop[d].wait_recv()
-        z_fwd[d].start()
 
     def assemble(w, carry):
         for t in range(TILES):
@@ -340,6 +343,9 @@
         return carry
 
     lax.fori_loop(0, WINDOW, assemble, 0)
+    for d in range(2):
+        z_hop[d].wait_recv()
+        z_fwd[d].start()
 
     def near_part(first, depth, low, high, initial=False):
         def columns(i, carry):
@@ -380,17 +386,17 @@
             xsend[l, low] = total[low * 16 : low * 16 + 16].astype(BF)
 
     for low in (1 - yl, yl):
-        for l, plane, slot in ((0, x2, xpar), (0, x3, xpar), (1, x1, 2)):
+        for l, plane, place in ((0, x2, xpar), (0, x3, xpar), (1, x1, 2)):
             rcopy(
                 xsend.at[l, low],
-                xin.at[slot, yl],
+                xin.at[place, yl],
                 x_s.at[0],
                 x_r.at[0],
                 dev(plane * 8 + z * 2 + low, yh, k),
             ).start()
     x_all = rcopy(xin, xin, x_s.at[0], x_r.at[0], dev(at_x(x1), yh, k))
-    for copy in near_halo:
-        copy.start()
+    for p in range(2):
+        near_halo[2 * p].start()
 
     @pl.when(edge)
     def _():
@@ -405,11 +411,22 @@
 
     mine = coeff.at[k, :, yh, z, yl]
     g_out = [
-        rcopy(mine, mine, g_s.at[i], g_r.at[i], target)
-        for i, target in enumerate((dev(flip, yh, k), dev(flip, oh, k), dev(r, oh, k)))
-    ]
-    for i in (2, 0, 1):
-        g_out[i].start()
+        rcopy(mine, mine, g_s.at[p], g_r.at[p], dev(flip, highs[p], k)) for p in range(2)
+    ]
+    g_fwd = []
+    for l in range(2):
+        theirs = coeff.at[k, l, highs[l], z, 1 - yl]
+        g_fwd.append(
+            rcopy(theirs, theirs, g_s.at[2 + l], g_r.at[2 + l], dev(flip, highs[1 - l], k))
+        )
+    for copy in g_out:
+        copy.start()
+    for p in range(2):
+        near_halo[2 * p + 1].start()
+    advance(PLAN[2])
+    for p in range(2):
+        g_out[p].wait_recv()
+        g_fwd[p].start()
 
     @pl.when(relays)
     def _():
@@ -418,8 +435,8 @@
             copy.start()
 
     forward_start(0)
-    advance(PLAN[2])
-    for copy in g_out:
+    advance(16 - done[0])
+    for copy in g_fwd:
         copy.wait_recv()
 
     def level(l, zz):
@@ -443,7 +460,6 @@
     for l in range(2):
         core_start(l, z)
     forward_start(1)
-    advance(16 - done[0])
     for copy in near_halo:
         copy.wait_recv()
     for copy in near_share:
@@ -452,6 +468,14 @@
         ring[d][0].wait_recv()
         ring[d][2].start()
         core_start(d, lasts[d])
+
+    @pl.when(edge)
+    def _():
+        for copy in far_halo:
+            copy.wait_recv()
+        for copy in far_share:
+            copy.start()
+
     for copy in near_share:
         copy.wait_recv()
     near_part(near_base, HALO, 0, 4)
@@ -459,27 +483,9 @@
         ring[d][1].wait_recv()
         core_start(1 - d, lasts[d])
 
-    @pl.when(edge)
-    def _():
-        for copy in far_halo:
-            copy.wait_recv()
-        for copy in far_share:
-            copy.start()
-
     for d in range(2):
         ring[d][2].wait_recv()
         core_start(d, zo)
-
-    @pl.when(edge)
-    def _():
-        for copy in far_share:
-            copy.wait()
-
-    @pl.when(jnp.logical_not(edge))
-    def _():
-        win[pl.ds(far_base, HALO), :] = jnp.zeros((HALO, N), BF)
-
-    near_part(far_base, HALO, 0, 4)
 
     def far_part(chips, low, count, target):
         blocks = [(a, l, h) for a in range(2) for l in range(2) for h in chips]
@@ -502,13 +508,24 @@
     for copy in swaps:
         copy.wait_recv()
     core_out.wait_recv()
-    far_part((yh,), HALF, HALF, acc)
+    far_part((yh,), 0, ROWS, acc)
+
+    @pl.when(edge)
+    def _():
+        for copy in far_share:
+            copy.wait()
+
+    @pl.when(jnp.logical_not(edge))
+    def _():
+        win[pl.ds(far_base, HALO), :] = jnp.zeros((HALO, N), BF)
+
+    near_part(far_base, HALO, 0, 4)
     for core in range(2):
         arrival(0, core).wait_recv()
-    far_part((0, 1), 0, HALF, out)
+    far_part((oh,), *BLOCKS[0], out)
     for core in range(2):
         arrival(1, core).wait_recv()
-    far_part((oh,), HALF, HALF, out)
+    far_part((oh,), *BLOCKS[1], out)
 
     for copy in (
         list(hop_all.values())
@@ -518,6 +535,7 @@
         + z_fwd
         + [x_all]
         + g_out
+        + g_fwd
         + ring[0]
         + ring[1]
         + [core_out]
@@ -561,8 +579,8 @@
         (3, 2),
         (1,),
         (1,),
-        (3,),
-        (3,),
+        (4,),
+        (4,),
         (2, 3),
         (2, 3),
         (1,),
@@ -586,7 +604,7 @@
             pltpu.VMEM((3, 2, 16, N), BF),
             pltpu.VMEM((2, 2, 2, 4, 2, 16, N), BF),
             pltpu.VMEM((2, 2, 2, ROWS, RB), BF),
-            pltpu.VMEM((2, 2, 2, 2, PIECE, RB), BF),
+            pltpu.VMEM((2, 2, 2, HALF, RB), BF),
             pltpu.VMEM((QUARTER, N), BF),
             pltpu.VMEM((ROWS, N), F32),
         ]

time: 50.7 us -> 52.6 us (1.037)
  the two profiles are of different devices: /device:TPU:3 before, /device:TPU:1 now
where the time goes in v4:
time: 52.6 us; the launch traced here: 52.4 us
  Pallas kernels  51.1 us (97%)
  local copies, waits for them, and re-layouts  1.32 us (3%)
    pallas_call x1, Pallas kernels, per_device(): pl.pallas_call(kernel, out_shape=pltpu.VMEM((ROWS, N), BF), in_specs=[pl....  51.1 us
    unnamed x1, local copies, waits for them, and re-layouts  1.32 us

profile of v4, /device:TPU:1, one launch (start us, length us, event | category | flops | bytes accessed | tf_op | source)
XLA Modules:
  0.0 52.4 jit_solution(15474677868951212697)
XLA Ops:
  0.0 51.1 %shard_map.73 = bf16[1024,1024]{1,0:T(8,128)(2,1)S(1)} custom-call(s32[4,16]{1,0:T(4,128)} %cols.1, bf16[4096,1024]{1,0:T(8,128)(2,1)} %vec.1, bf16[4,16,256,256]{3,2,1,0:T(8,128)(2,1)} %near.1, bf16[4096,128]{1,0:T(8,128)(2,1)} %left_one.1, bf16[4096,128]{1,0:T(8,128)(2,1)} %left_two.1, bf16[4096,128]{1,0:T(8,128)(2,1)} %right_one.1, ...), custom_call_target="tpu_custom_call" | custom-call | tf_op jit(solution)/shard_map/pallas_call | solution.py:589
  51.1 1.3 %copy.9 = bf16[1024,1024]{1,0:T(8,128)(2,1)} copy(bf16[1024,1024]{1,0:T(8,128)(2,1)S(1)} %shard_map.73) | data formatting | bytes 4194304

commit v5 on v4

--- a/solution.py
+++ b/solution.py
@@ -19,10 +19,10 @@
 RB = 128
 HALF = ROWS // 2
 BLOCKS = ((0, 768), (768, 256))
-SPLIT = ((80, 32), (112, 32))
+SPLIT = ((48, 64), (80, 64))
 STEPS = 8
-EARLY = 1
-PLAN = (5, 5, 3)
+EARLY = 2
+PLAN = (5, 5, 5)
 BF = jnp.bfloat16
 F32 = jnp.float32
 
@@ -127,6 +127,7 @@
         dev(flip, oh, k),
         dev(flip, yh, ok),
         dev(flip, oh, ok),
+        dev(r, oh, k),
         other,
         dev(at_z(zp), yh, k),
         dev(at_z(zm), yh, k),
@@ -411,22 +412,15 @@
 
     mine = coeff.at[k, :, yh, z, yl]
     g_out = [
-        rcopy(mine, mine, g_s.at[p], g_r.at[p], dev(flip, highs[p], k)) for p in range(2)
-    ]
-    g_fwd = []
-    for l in range(2):
-        theirs = coeff.at[k, l, highs[l], z, 1 - yl]
-        g_fwd.append(
-            rcopy(theirs, theirs, g_s.at[2 + l], g_r.at[2 + l], dev(flip, highs[1 - l], k))
-        )
-    for copy in g_out:
-        copy.start()
+        rcopy(mine, mine, g_s.at[i], g_r.at[i], target)
+        for i, target in enumerate((dev(flip, yh, k), dev(flip, oh, k), dev(r, oh, k)))
+    ]
+    for i in (2, 0, 1):
+        g_out[i].start()
+
     for p in range(2):
         near_halo[2 * p + 1].start()
     advance(PLAN[2])
-    for p in range(2):
-        g_out[p].wait_recv()
-        g_fwd[p].start()
 
     @pl.when(relays)
     def _():
@@ -436,7 +430,7 @@
 
     forward_start(0)
     advance(16 - done[0])
-    for copy in g_fwd:
+    for copy in g_out:
         copy.wait_recv()
 
     def level(l, zz):
@@ -482,10 +476,20 @@
     for d in range(2):
         ring[d][1].wait_recv()
         core_start(1 - d, lasts[d])
-
     for d in range(2):
         ring[d][2].wait_recv()
         core_start(d, zo)
+
+    @pl.when(edge)
+    def _():
+        for copy in far_share:
+            copy.wait()
+
+    @pl.when(jnp.logical_not(edge))
+    def _():
+        win[pl.ds(far_base, HALO), :] = jnp.zeros((HALO, N), BF)
+
+    near_part(far_base, HALO, 0, 4)
 
     def far_part(chips, low, count, target):
         blocks = [(a, l, h) for a in range(2) for l in range(2) for h in chips]
@@ -509,17 +513,6 @@
         copy.wait_recv()
     core_out.wait_recv()
     far_part((yh,), 0, ROWS, acc)
-
-    @pl.when(edge)
-    def _():
-        for copy in far_share:
-            copy.wait()
-
-    @pl.when(jnp.logical_not(edge))
-    def _():
-        win[pl.ds(far_base, HALO), :] = jnp.zeros((HALO, N), BF)
-
-    near_part(far_base, HALO, 0, 4)
     for core in range(2):
         arrival(0, core).wait_recv()
     far_part((oh,), *BLOCKS[0], out)
@@ -535,7 +528,6 @@
         + z_fwd
         + [x_all]
         + g_out
-        + g_fwd
         + ring[0]
         + ring[1]
         + [core_out]
@@ -579,8 +571,8 @@
         (3, 2),
         (1,),
         (1,),
-        (4,),
-        (4,),
+        (3,),
+        (3,),
         (2, 3),
         (2, 3),
         (1,),

time: 52.6 us -> 49.9 us (0.949)
  the two profiles are of different devices: /device:TPU:1 before, /device:TPU:3 now
where the time goes in v5:
time: 49.9 us; the launch traced here: 49.3 us
  Pallas kernels  48 us (96%)
  local copies, waits for them, and re-layouts  1.32 us (3%)
    pallas_call x1, Pallas kernels, per_device(): pl.pallas_call(kernel, out_shape=pltpu.VMEM((ROWS, N), BF), in_specs=[pl....  48 us
    unnamed x1, local copies, waits for them, and re-layouts  1.32 us

profile of v5, /device:TPU:3, one launch (start us, length us, event | category | flops | bytes accessed | tf_op | source)
XLA Modules:
  0.0 49.3 jit_solution(7716028677343308119)
XLA Ops:
  0.0 48.0 %shard_map.73 = bf16[1024,1024]{1,0:T(8,128)(2,1)S(1)} custom-call(s32[4,16]{1,0:T(4,128)} %cols.1, bf16[4096,1024]{1,0:T(8,128)(2,1)} %vec.1, bf16[4,16,256,256]{3,2,1,0:T(8,128)(2,1)} %near.1, bf16[4096,128]{1,0:T(8,128)(2,1)} %left_one.1, bf16[4096,128]{1,0:T(8,128)(2,1)} %left_two.1, bf16[4096,128]{1,0:T(8,128)(2,1)} %right_one.1, ...), custom_call_target="tpu_custom_call" | custom-call | tf_op jit(solution)/shard_map/pallas_call | solution.py:581
  48.0 1.3 %copy.9 = bf16[1024,1024]{1,0:T(8,128)(2,1)} copy(bf16[1024,1024]{1,0:T(8,128)(2,1)S(1)} %shard_map.73) | data formatting | bytes 4194304
